TPU v7x, 32 devices: a whole 2x2x4 slice. The times are simulated.
32 devices in a mesh: dp: 4 (over y, core), fsdp: 8 (over z, x).
Axes of the slice: x: 2, y: 2, z: 4, core: 2. Of those that a mesh axis runs over, the one named last changes fastest.
Arguments:
- hidden_in: bfloat16 [2, 32, 128, 1024], P(None, ('dp', 'fsdp')), may hold values from -6 to 6
- memory: bfloat16 [2, 32, 588, 1024], P(None, ('dp', 'fsdp')), may hold values from -6 to 6
- cotangent: bfloat16 [2, 32, 128, 1024], P(None, ('dp', 'fsdp')), may hold values from -6 to 6
- lengths: int32 [2, 32], P(None, ('dp', 'fsdp')), may hold values from 32 to 128, as said below
- memory_count: int32 [2, 32], P(None, ('dp', 'fsdp')), may hold values from 147 to 588, as said below
- causal_gain: bfloat16 [1024], P(('dp', 'fsdp')), may hold values from 0.5 to 1.5
- causal_query: bfloat16 [1024, 1024], P(('dp', 'fsdp')), may hold values from -0.1875 to 0.1875
- causal_key: bfloat16 [1024, 1024], P(('dp', 'fsdp')), may hold values from -0.1875 to 0.1875
- causal_value: bfloat16 [1024, 1024], P(('dp', 'fsdp')), may hold values from -0.1875 to 0.1875
- causal_output: bfloat16 [1024, 1024], P(('dp', 'fsdp')), may hold values from -1.5 to 1.5
- source_gain: bfloat16 [1024], P(('dp', 'fsdp')), may hold values from 0.5 to 1.5
- source_query: bfloat16 [1024, 1024], P(('dp', 'fsdp')), may hold values from -0.1875 to 0.1875
- source_key: bfloat16 [1024, 1024], P(('dp', 'fsdp')), may hold values from -0.1875 to 0.1875
- source_value: bfloat16 [1024, 1024], P(('dp', 'fsdp')), may hold values from -0.1875 to 0.1875
- source_output: bfloat16 [1024, 1024], P(('dp', 'fsdp')), may hold values from -1.5 to 1.5
- dense_gain: bfloat16 [1024], P(('dp', 'fsdp')), may hold values from 0.5 to 1.5
- dense_expand: bfloat16 [1024, 4096], P(('dp', 'fsdp')), may hold values from -0.1875 to 0.1875
- dense_reduce: bfloat16 [4096, 1024], P(('dp', 'fsdp')), may hold values from -0.09375 to 0.09375
Outputs:
- hidden_out: bfloat16 [2, 32, 128, 1024], P(None, ('dp', 'fsdp'))
- input_gradient: float32 [2, 32, 128, 1024], P(None, ('dp', 'fsdp'))
- memory_gradient: float32 [2, 32, 588, 1024], P(None, ('dp', 'fsdp'))
- causal_gain_gradient: float32 [1024], P(('dp', 'fsdp'))
- causal_query_gradient: float32 [1024, 1024], P(('dp', 'fsdp'))
- causal_key_gradient: float32 [1024, 1024], P(('dp', 'fsdp'))
- causal_value_gradient: float32 [1024, 1024], P(('dp', 'fsdp'))
- causal_output_gradient: float32 [1024, 1024], P(('dp', 'fsdp'))
- source_gain_gradient: float32 [1024], P(('dp', 'fsdp'))
- source_query_gradient: float32 [1024, 1024], P(('dp', 'fsdp'))
- source_key_gradient: float32 [1024, 1024], P(('dp', 'fsdp'))
- source_value_gradient: float32 [1024, 1024], P(('dp', 'fsdp'))
- source_output_gradient: float32 [1024, 1024], P(('dp', 'fsdp'))
- dense_gain_gradient: float32 [1024], P(('dp', 'fsdp'))
- dense_expand_gradient: float32 [1024, 4096], P(('dp', 'fsdp'))
- dense_reduce_gradient: float32 [4096, 1024], P(('dp', 'fsdp'))
Inputs may be any that keep to these rules, and one draw needn't show every extreme that they name: `lengths`: each micro-batch has a page of exactly 128 tokens. `memory_count`: each value is 147 or 588; both occur in every draw.
All inputs are finite; a program needn't handle non-finite values.
Results may differ from a plain program's by a relative error of at most 0.019.
Values may be sent and summed in bfloat16 or wider, within the bound.
A program may use at most 384 MiB of HBM per device.

v0:
```python
import functools

import jax
import jax.numpy as jnp
from jax import lax
from jax.experimental import pallas as pl
from jax.experimental.pallas import tpu as pltpu
from jax.sharding import PartitionSpec as P

HD = 64
EPS = 1e-05
AXES = ("dp", "fsdp")
CORES = 2
WIDTH = 1024
BLOCK = 256
MESH = pl.DeviceIdType.MESH


class Grid:
    def __init__(self):
        dp, fsdp = lax.axis_size("dp"), lax.axis_size("fsdp")
        self.n = dp // CORES
        self.depth = fsdp // self.n
        self.devices = dp * fsdp
        d, f = lax.axis_index("dp"), lax.axis_index("fsdp")
        self.at = (d // CORES, d % CORES, f // self.n, f % self.n)

    def device(self, y, c, z, x):
        return (y * CORES + c, z * self.n + x)

    def step_z(self, k):
        y, c, z, x = self.at
        return self.device(y, c, lax.rem(z + k, self.depth), x)

    def step_plane(self, k, swap):
        y, c, z, x = self.at
        odd = lax.rem(c + swap, 2)
        return self.device(
            lax.rem(y + k * odd, self.n), c, z, lax.rem(x + k * (1 - odd), self.n)
        )

    def partner(self):
        y, c, z, x = self.at
        return self.device(y, 1 - c, z, x)

    def place(self, a, b):
        y, c, z, x = self.at
        ky = a * c + b * (1 - c)
        kx = a * (1 - c) + b * c
        return lax.rem(y + ky, self.n), lax.rem(x + kx, self.n)

    def peers(self):
        line = [self.step_z(k) for k in range(1, self.depth)]
        plane = [self.step_plane(k, s) for s in (0, 1) for k in range(1, self.n)]
        return line + plane + [self.partner()]

    def meet(self):
        barrier = pltpu.get_barrier_semaphore()
        peers = self.peers()
        for peer in peers:
            pl.semaphore_signal(barrier, inc=1, device_id=peer, device_id_type=MESH)
        pl.semaphore_wait(barrier, len(peers))


def remote(src, dst, send_sem, recv_sem, device):
    return pltpu.make_async_remote_copy(
        src_ref=src,
        dst_ref=dst,
        send_sem=send_sem,
        recv_sem=recv_sem,
        device_id=device,
        device_id_type=MESH,
    )


def started(*copy):
    made = remote(*copy)
    made.start()
    return made


class Plan:
    def __init__(self):
        self.calls = {}

    def add(self, tick, rank, call, *args):
        self.calls.setdefault((tick, rank), []).append((call, args))

    def run(self):
        for key in sorted(self.calls):
            for call, args in self.calls[key]:
                call(*args)


def times(left, right):
    return jnp.dot(left, right, preferred_element_type=jnp.float32)


def times_transposed(left, right):
    return lax.dot_general(left, right, (((1,), (1,)), ((), ())), preferred_element_type=jnp.float32)


def transposed_times(left, right):
    return lax.dot_general(left, right, (((0,), (0,)), ((), ())), preferred_element_type=jnp.float32)


def standardize(value):
    centred = value - jnp.mean(value, axis=-1, keepdims=True)
    spread = jnp.mean(centred * centred, axis=-1, keepdims=True)
    row_scale = lax.rsqrt(spread + EPS)
    return centred * row_scale, row_scale


def standardize_back(grad, unit, row_scale, gain):
    grad_unit = grad * gain
    inner = jnp.mean(grad_unit * unit, axis=-1, keepdims=True)
    return row_scale * (grad_unit - jnp.mean(grad_unit, axis=-1, keepdims=True) - unit * inner)


def lane_window(col, pair):
    return pl.ds(pl.multiple_of(col + pair * 2 * HD, 2 * HD), 2 * HD)


def both_heads(lane, value):
    zero = jnp.zeros_like(value)
    return jnp.concatenate(
        [jnp.where(lane < HD, value, zero), jnp.where(lane < HD, zero, value)], axis=0
    )


def causal(length, live):
    key = lax.broadcasted_iota(jnp.int32, (length, 2 * length), 0)
    query = lax.rem(lax.broadcasted_iota(jnp.int32, (length, 2 * length), 1), length)
    return (key <= query) & (key < live)


STRIP = 32


def strips(count, body, carry=None):
    def one(k, carry):
        return body(pl.ds(pl.multiple_of(k * STRIP, STRIP), STRIP), carry)

    return lax.fori_loop(0, count // STRIP, one, carry)


def bands(count, body):
    def one(k, carry):
        body(pl.multiple_of(k * 2 * BLOCK, BLOCK))
        return carry

    lax.fori_loop(0, count // (2 * BLOCK), one, 0)


FLAT_AHEAD = 2
TALL_GAP = 1


def front_kernel(dims, chunks, names_, n_src, *refs):
    pages, length, slots = dims
    n_out = len(names_)
    it = iter(refs)

    def take(k):
        return [next(it) for _ in range(k)]

    shards = take(n_src)
    x_in, cot_in, memory_in, counts, lengths = take(5)
    outs = take(n_out)
    saved_out = take(13)
    gains, lse_cross, lse_self = take(3)
    saved = take(13)
    (result, hidden, pre, third, after_cross, cctx, second, cq, kv, after_self, ctx, first, qkv) = saved
    x_bf, cot, memory, w_a, w_b, w_d, w_gain, total_out, g_hidden = take(9)
    local, zs, zr, ps, pr, qs, qr, cs, cr, us, ur, ds, dr, loads_sem, stores_sem = take(15)
    f32, bf16 = jnp.float32, jnp.bfloat16
    grid = Grid()
    n, depth = grid.n, grid.depth
    y, c, z, x = grid.at
    tokens, D = x_bf.shape
    loads = {}

    def fetch(name, src, dst, slot):
        loads[name] = pltpu.make_async_copy(src, dst, loads_sem.at[slot])
        loads[name].start()

    def need(*names):
        for name in names:
            copy = loads.pop(name, None)
            if copy is not None:
                copy.wait()

    fetch("x", x_in, x_bf, 0)
    fetch("cot", cot_in, cot, 1)
    fetch("memory", memory_in, memory, 2)
    grid.meet()
    pending = []

    def send(*copy):
        made = started(*copy)
        pending.append(made)
        return made

    def window(i):
        _, r0, nr, c0, nc, _, o0, _ = chunks[i]
        return pl.ds(r0, nr), pl.ds(o0, nc)

    def out(i):
        return outs[chunks[i][5]]

    def shard(i):
        m, r0, nr, c0, nc, _, _, _ = chunks[i]
        return shards[m].at[pl.ds(r0, nr), pl.ds(c0, nc)]

    def block(i, yy, zz, xx):
        return out(i).at[(yy, c, zz, xx) + window(i)]

    def back(a, b):
        return grid.place((n - a) % n, (n - b) % n)

    def column(i, a, b):
        yy, xx = back(a, b)
        return out(i).at[(yy, c, slice(None), xx) + window(i)]

    def share(i, a, b):
        piece = column(i, a, b)
        slot = a * n + b
        return send(piece, piece, cs.at[i, slot], cr.at[i, slot], grid.partner())

    zc, pc, qc, cc, lc = {}, {}, {}, {}, {}

    def keep_own(i):
        lc[i] = pltpu.make_async_copy(shard(i), block(i, y, z, x), local.at[i])
        lc[i].start()

    def stage_z(i):
        zc[i] = [
            send(shard(i), block(i, y, z, x), zs.at[i, k - 1], zr.at[i, k - 1], grid.step_z(k))
            for k in range(1, depth)
        ]
        keep_own(i)

    def stage_p(i):
        for copy in zc[i]:
            copy.wait_recv()
        lc[i].wait()
        piece = column(i, 0, 0)
        pc[i] = [
            send(piece, piece, ps.at[i, a - 1], pr.at[i, a - 1], grid.step_plane(a, 0))
            for a in range(1, n)
        ]
        qc[i] = [
            send(piece, piece, qs.at[i, b - 1], qr.at[i, b - 1], grid.step_plane(b, 1))
            for b in range(1, n)
        ]
        cc[i] = [share(i, 0, 0)]

    def stage_q(i):
        for a in range(1, n):
            pc[i][a - 1].wait_recv()
            piece = column(i, a, 0)
            for b in range(1, n):
                j = a * (n - 1) + b - 1
                qc[i].append(
                    send(piece, piece, qs.at[i, j], qr.at[i, j], grid.step_plane(b, 1))
                )
            cc[i].append(share(i, a, 0))

    def stage_c(i):
        j = 0
        for a in range(n):
            for b in range(1, n):
                qc[i][j].wait_recv()
                j += 1
                cc[i].append(share(i, a, b))

    def tall_p(i):
        keep_own(i)
        pc[i] = [
            send(shard(i), block(i, y, z, x), ps.at[i, a - 1], pr.at[i, a - 1], grid.step_plane(a, 0))
            for a in range(1, n)
        ]

    def tall_q(i):
        lc[i].wait()
        qc[i] = []
        for a in range(n):
            if a:
                pc[i][a - 1].wait_recv()
            yy, xx = back(a, 0)
            piece = block(i, yy, z, xx)
            for b in range(1, n):
                j = a * (n - 1) + b - 1
                qc[i].append(
                    send(piece, piece, qs.at[i, j], qr.at[i, j], grid.step_plane(b, 1))
                )

    def layer(i, k, j):
        zz = lax.rem(z + (depth - j if k == 0 else j), depth)
        return out(i).at[(slice(None), c, zz, slice(None)) + window(i)]

    def hop(i, k, j):
        piece = layer(i, k, j)
        send_sem, recv_sem = ((us, ur), (ds, dr))[k]
        to = grid.device(y, c, lax.rem(z + (1 if k == 0 else depth - 1), depth), x)
        return remote(piece, piece, send_sem.at[i, j], recv_sem.at[i, j], to)

    def share_layer(i, k, j):
        piece = layer(i, k, j)
        slot = k * (depth - 1) + j
        return remote(piece, piece, cs.at[i, slot], cr.at[i, slot], grid.partner())

    def level(k):
        return z if k == 0 else depth - 1 - z

    def climb(i, j):
        if j == 0:
            for copy in qc[i]:
                copy.wait_recv()
            share_layer(i, 0, 0).start()
        for k in (0, 1):
            if j:

                @pl.when(level(k) >= j)
                def _():
                    hop(i, k, j - 1).wait_recv()
                    share_layer(i, k, j).start()

            if j < depth - 1:

                @pl.when((level(k) >= j) & (level(k) < depth - 1))
                def _():
                    hop(i, k, j).start()

    def each_layer(i, call, hops):
        call(share_layer(i, 0, 0))
        for k in (0, 1):
            for j in range(depth - 1):
                if hops:

                    @pl.when((level(k) >= j) & (level(k) < depth - 1))
                    def _():
                        call(hop(i, k, j))

                @pl.when(level(k) >= j + 1)
                def _():
                    call(share_layer(i, k, j + 1))

    there = set()

    def arrive(*ids):
        for i in ids:
            if i in there:
                continue
            there.add(i)
            if chunks[i][7]:
                each_layer(i, lambda copy: copy.wait_recv(), False)
            else:
                for copy in cc[i]:
                    copy.wait_recv()

    def pull(name, k, dst, slot):
        ids = held[name][k]
        arrive(*ids)
        fetch((name, k), out(ids[0]), dst, slot)

    def store(name, slot):
        src = saved[name]
        made = pltpu.make_async_copy(src, saved_out[name], stores_sem.at[slot])
        made.start()
        stores.append(made)

    stores = []
    lane = lax.broadcasted_iota(jnp.int32, (length, 2 * HD), 1)

    def attention(page, pair, q_ref, k_ref, k_row, k_rows, k_col, v_col, allowed, to, lse):
        q_at, k_at = pl.ds(page * length, length), pl.ds(k_row, k_rows)
        q = both_heads(lane, q_ref[q_at, lane_window(0, pair)])
        keys = k_ref[k_at, lane_window(k_col, pair)]
        values = k_ref[k_at, lane_window(v_col, pair)]
        scores = times_transposed(keys, q) * HD ** (-0.5)
        scores = jnp.where(allowed, scores, -1000000000.0)
        top = jnp.max(scores, axis=0, keepdims=True)
        expos = jnp.exp(scores - top)
        sum_ = jnp.sum(expos, axis=0, keepdims=True)
        probs = (expos * (1.0 / sum_)).astype(bf16)
        lse[pl.ds(page * (D // HD // 2) + pair, 1), :] = top + jnp.log(sum_)
        found = transposed_times(probs, values)
        to[q_at, lane_window(0, pair)] = jnp.where(lane < HD, found[:length], found[length:]).astype(bf16)

    def read_gains():
        arrive(*held["gain"][0])
        copy = pltpu.make_async_copy(out(held["gain"][0][0]), w_gain, loads_sem.at[3])
        copy.start()
        copy.wait()
        columns = w_gain.reshape(D, 128)[...].astype(f32)
        gains[...] = columns.T[:8]

    def project(left, weight, col, count, to, to_col):
        def body(at):
            w_at = pl.ds(pl.multiple_of(col + at, BLOCK), 2 * BLOCK)
            to_at = pl.ds(pl.multiple_of(to_col + at, BLOCK), 2 * BLOCK)
            to[:, to_at] = times(left[...], weight[:, w_at]).astype(to.dtype)

        bands(count, body)

    def first_norm():
        need("x")
        gain = gains[pl.ds(0, 1), :]

        def body(at, carry):
            unit, _ = standardize(x_bf[at].astype(f32))
            first[at] = (unit * gain).astype(bf16)
            return carry

        strips(tokens, body, 0)

    def self_project(k):
        need(("self", k))
        project(first, flat_b, k * D, D, qkv, k * D)

    def self_attention(page):
        allowed = causal(length, lengths[page])

        def body(pair, carry):
            attention(page, pair, qkv, qkv, page * length, length, D, 2 * D, allowed, ctx, lse_self)
            return carry

        lax.fori_loop(0, D // (2 * HD), body, 0)

    def residual(left, weight, col, base, to):
        def body(at):
            here = pl.ds(at, 2 * BLOCK)
            w_at = pl.ds(pl.multiple_of(col + at, BLOCK), 2 * BLOCK)
            to[:, here] = base[:, here].astype(f32) + times(left[...], weight[:, w_at])

        bands(D, body)

    def self_out():
        need(("self", 3))
        residual(ctx, flat_b, 3 * D, x_bf, after_self)
        gain = gains[pl.ds(1, 1), :]

        def body(at, carry):
            unit, _ = standardize(after_self[at])
            second[at] = (unit * gain).astype(bf16)
            return carry

        strips(tokens, body, 0)

    def memory_project(page, part):
        need("memory", ("kv", 0), ("kv", 1))
        span = -(-slots // 32) * 16
        at = pl.ds(page * slots + part * span, min(span, slots - part * span))

        def body(col):
            here = pl.ds(col, 2 * BLOCK)
            kv[at, here] = times(memory[at, :], flat_a[:, here]).astype(bf16)

        bands(2 * D, body)

    def cross_query():
        need(("qo", 0))
        project(second, flat_a, 0, D, cq, 0)

    def cross_attention(page, part):
        allowed = lax.broadcasted_iota(jnp.int32, (slots, 2 * length), 0) < counts[page]
        pairs = D // (2 * HD) // 2

        def body(k, carry):
            pair = part * pairs + k
            attention(page, pair, cq, kv, page * slots, slots, 0, D, allowed, cctx, lse_cross)
            return carry

        lax.fori_loop(0, pairs, body, 0, unroll=2)

    def cross_out():
        need(("qo", 1))
        residual(cctx, flat_a, D, after_self, after_cross)
        gain = gains[pl.ds(2, 1), :]

        def body(at, carry):
            unit, _ = standardize(after_cross[at])
            third[at] = (unit * gain).astype(bf16)
            return carry

        strips(tokens, body, 0)

    def hidden_grad(k):
        need("cot", ("reduce", 0))

        def body(at):
            here = pl.ds(pl.multiple_of(k * D + at, BLOCK), 2 * BLOCK)
            g_hidden[:, here] = times_transposed(cot[...], flat_d[here, :])

        bands(D, body)

    def expand(k):
        need(("expand", k))

        def body(j, carry):
            at = pl.ds(pl.multiple_of(k * D + j * 2 * BLOCK, BLOCK), 2 * BLOCK)
            value = times(third[...], flat_b[:, at])
            below = 0.5 + 0.5 * lax.erf(value * 0.5**0.5)
            hidden[:, at] = (value * below).astype(bf16)
            density = jnp.exp(-0.5 * value * value) * 0.3989422804014327
            pre[:, at] = (g_hidden[:, at] * (below + value * density)).astype(bf16)
            return carry

        lax.fori_loop(0, D // (2 * BLOCK), body, 0)

    def reduce_out(k):
        at = pl.ds(k * D, D)

        def body(col):
            here = pl.ds(col, 2 * BLOCK)
            value = after_cross[:, here] if k == 0 else total_out[:, here]
            value = value + times(hidden[:, at], flat_d[at, here])
            if k < 3:
                total_out[:, here] = value
            else:
                result[:, here] = value.astype(bf16)

        bands(D, body)

    flat_a, flat_b, flat_d = w_a.reshape(D, 2 * D), w_b.reshape(D, 4 * D), w_d.reshape(4 * D, D)

    held = {}
    for i, chunk in enumerate(chunks):
        name, k = names_[chunk[5]]
        held.setdefault(name, {}).setdefault(k, []).append(i)

    plan = Plan()
    flat = [i for i, chunk in enumerate(chunks) if not chunk[7]]
    tall = [i for i, chunk in enumerate(chunks) if chunk[7]]
    tick = {}
    for t, i in enumerate(flat):
        plan.add(t - FLAT_AHEAD, 0, stage_z, i)
        plan.add(t, 2, stage_p, i)
        plan.add(t + 1, 4, stage_q, i)
        plan.add(t + 2, 6, stage_c, i)
        tick[i] = t + 3
    for t, i in enumerate(tall):
        t = TALL_GAP * t - 1
        plan.add(t, 1, tall_p, i)
        plan.add(t + 2, 3, tall_q, i)
        for h in range(depth):
            plan.add(t + 4 + 2 * h, 5, climb, i, h)
        tick[i] = t + 4 + 2 * (depth - 1) + 1

    def ready(name, k):
        return max(tick[i] for i in held[name][k])

    def part(buffer, k, width):
        return buffer.at[:, :, :, :, :, pl.ds(k * width, width)]

    clock = [0]

    def then(when, call, *args):
        clock[0] = max(clock[0] + 1, 3 * when)
        plan.add(clock[0] // 3, 3 + 2 * (clock[0] % 3), call, *args)
        return clock[0] // 3

    def keep(*names):
        for name in names:
            store(name, name)

    plan.add(ready("gain", 0), 8, read_gains)
    plan.add(ready("gain", 0), 8, first_norm)
    for k in range(2):
        plan.add(ready("kv", k), 8, pull, "kv", k, part(w_a, k, D), 8 + k)
    for k in range(4):
        plan.add(ready("self", k), 8, pull, "self", k, part(w_b, k, D), 4 + k)
    for page in range(pages):
        for half in range(2):
            kv_done = then(ready("kv", 1) + 1, memory_project, page, half)
    for k in range(3):
        then(ready("self", k) + 1, self_project, k)
    for page in range(pages):
        then(0, self_attention, page)
    self_done = then(ready("self", 3) + 1, self_out)
    plan.add(self_done, 9, keep, 8, 10, 11, 12, 9, 6)
    for k in range(2):
        plan.add(max(ready("qo", k), kv_done + 1), 8, pull, "qo", k, part(w_a, k, D), 10 + k)
    for k in range(4):
        plan.add(
            max(ready("expand", k), self_done + 1), 8, pull, "expand", k, part(w_b, k, D), 12 + k
        )
    plan.add(ready("reduce", 0), 8, pull, "reduce", 0, w_d, 16)
    then(max(ready("qo", 0), kv_done + 1) + 1, cross_query)
    for page in range(pages):
        for half in range(2):
            then(0, cross_attention, page, half)
    cross_done = then(max(ready("qo", 1), kv_done + 1) + 1, cross_out)
    plan.add(cross_done, 9, keep, 3, 4, 5, 7)
    for k in range(4):
        plan.add(ready("reduce", 0) + 1 + k // 2, 9, hidden_grad, k)
    for k in range(4):
        then(max(ready("expand", k), self_done + 1) + 1, expand, k)
        last = then(0, reduce_out, k)
    plan.add(last, 10, keep, 1, 2, 0)
    plan.run()
    for i in flat:
        arrive(i)
    for i in tall:
        arrive(i)
        each_layer(i, lambda copy: copy.wait_send(), True)
    for copy in pending:
        copy.wait_send()
    for copy in stores:
        copy.wait()


def front(sources, pieces, names, tokens_in, shapes):
    dp, fsdp = lax.axis_size("dp"), lax.axis_size("fsdp")
    n = dp // CORES
    depth = fsdp // n
    rows = sources[0].shape[0]
    pages, length, slots = shapes
    tokens, D = pages * length, WIDTH
    groups = [(4 * rows if name == "reduce" else rows, 128 if name == "gain" else D) for name, _ in names]
    chunks = [(m, r0, rows, c0, groups[o][1], o, 0, tall) for m, r0, c0, o, tall in pieces]
    t = len(chunks)
    slot_count = max(n * n, 2 * depth - 1)
    shapes_ = (depth - 1, depth - 1, n - 1, n - 1, n * (n - 1), n * (n - 1), slot_count, slot_count)
    shapes_ += (depth - 1,) * 4
    dma = pltpu.SemaphoreType.DMA
    f32, bf16 = jnp.float32, jnp.bfloat16
    lead = (n, CORES, depth, n)
    saved = [
        ((tokens, D), bf16),
        ((tokens, 4 * D), bf16),
        ((tokens, 4 * D), bf16),
        ((tokens, D), bf16),
        ((tokens, D), f32),
        ((tokens, D), bf16),
        ((tokens, D), bf16),
        ((tokens, D), bf16),
        ((pages * slots, 2 * D), bf16),
        ((tokens, D), f32),
        ((tokens, D), bf16),
        ((tokens, D), bf16),
        ((tokens, 3 * D), bf16),
    ]
    small = [((8, D), f32)] + [((pages * D // HD // 2, 2 * length), f32)] * 2
    hbm = pl.BlockSpec(memory_space=pltpu.HBM)
    vmem = pl.BlockSpec(memory_space=pltpu.VMEM)
    smem = pl.BlockSpec(memory_space=pltpu.SMEM)
    found = pl.pallas_call(
        functools.partial(front_kernel, shapes, chunks, names, len(sources)),
        out_shape=[jax.ShapeDtypeStruct(lead + g, bf16) for g in groups]
        + [jax.ShapeDtypeStruct(*s) for s in saved + small],
        in_specs=[vmem] * len(sources) + [hbm] * 3 + [smem] * 2,
        out_specs=[hbm] * (len(groups) + len(saved)) + [vmem] * 3,
        scratch_shapes=[pltpu.VMEM(*s) for s in saved]
        + [
            pltpu.VMEM((tokens, D), bf16),
            pltpu.VMEM((tokens, D), bf16),
            pltpu.VMEM((pages * slots, D), bf16),
            pltpu.VMEM(lead + (rows, 2 * D), bf16),
            pltpu.VMEM(lead + (rows, 4 * D), bf16),
            pltpu.VMEM(lead + (4 * rows, D), bf16),
            pltpu.VMEM(lead + (rows, 128), bf16),
            pltpu.VMEM((tokens, D), f32),
            pltpu.VMEM((tokens, 4 * D), f32),
            dma((t,)),
        ]
        + [dma((t, k)) for k in shapes_]
        + [dma((20,)), dma((13,))],
        compiler_params=pltpu.CompilerParams(
            collective_id=0, has_side_effects=True, vmem_limit_bytes=67043328
        ),
    )(*sources, *tokens_in)
    weights = [
        w.reshape(dp * fsdp * g[0], g[1]) for w, g in zip(found[: len(groups)], groups)
    ]
    return weights, found[len(groups) : len(groups) + len(saved)], found[len(groups) + len(saved) :]


RING = 4
KEPT = (("self", 4), ("kv", 2), ("qo", 2), ("expand", 4))
SPARE = 2
BACK_TALL = (1, 5, 9)
TALL_STEP = 2


def back_kernel(dims, *refs):
    pages, length, slots = dims
    it = iter(refs)

    def take(k):
        return [next(it) for _ in range(k)]

    (hidden_in, pre_in, third_in, out_in, cross_in, cctx_in, second_in, cq_in, kv_in, memory_in,
     self_in, ctx_in, first_in, qkv_in, x_in) = take(15)
    kept = {name: take(count) for name, count in KEPT}
    counts, lengths, gains, lse_cross, lse_self = take(5)
    grad_outs = take(7)
    gain_out, input_out, memory_out = take(3)
    (hidden, pre, third, out_grad, cross, cctx, second, cq, kv, memory, after_self, ctx, first, qkv,
     w_a, w_b, branch, g_ctx, stage, g_norm) = take(20)
    send0, got0, parts, got1, halves, got2, line, got3, gain_sum, gain_got = take(10)
    tower, tower_got, tower_got1, tower_half, tower_got2 = take(5)
    local, s0, r0, s1, r1, s2, r2, s3, r3, gs, gr, free, free1 = take(13)
    sz, rz, sa, ra, sb, rb = take(6)

    grid = Grid()
    n, depth = grid.n, grid.depth
    y, c, z, x = grid.at
    rows, width = send0.shape[-2:]
    f32, bf16 = jnp.float32, jnp.bfloat16
    copies, loads = {}, {}

    def fetch(name, src, dst, slot):
        loads[name] = pltpu.make_async_copy(src, dst, local.at[slot])
        loads[name].start()

    def need(*names):
        for name in names:
            copy = loads.pop(name, None)
            if copy is not None:
                copy.wait()

    D = third.shape[1]
    fetch("hidden", hidden_in, hidden, 0)
    fetch("out", out_in, out_grad, 1)
    fetch("pre", pre_in, pre, 2)
    fetch("third", third_in, third, 3)

    def weights(label, *moves):
        for name, k, buffer, half in moves:
            slot = 15 + half + (0 if buffer is w_a else 2)
            fetch((label, slot), kept[name][k], buffer.at[:, pl.ds(half * D, D)], slot)

    def need_all(label):
        need(*[key for key in list(loads) if key[0] == label])

    weights("expand", *[("expand", k, (w_a, w_b)[k // 2], k % 2) for k in range(4)])
    fetch("cross", cross_in, cross, 4)
    grid.meet()
    fetch("cctx", cctx_in, cctx, 5)
    fetch("cq", cq_in, cq, 7)
    fetch("kv", kv_in, kv, 8)
    fetch("second", second_in, second, 6)
    fetch("memory", memory_in, memory, 9)
    fetch("self", self_in, after_self, 10)
    fetch("ctx", ctx_in, ctx, 11)
    fetch("first", first_in, first, 12)
    fetch("qkv", qkv_in, qkv, 13)

    chunks = []
    wide = hidden.shape[1] // grid.devices
    for col in range(0, D, width * rows // wide):
        chunks.append((0, hidden, out_grad, col, ("hidden", "out")))
    for col in range(0, pre.shape[1], width):
        chunks.append((1, third, pre, col, ("third", "pre")))
    OUT_CHUNK = len(chunks)
    chunks.append((2, cctx, branch, 0, ("cctx",)))
    chunks.append((3, second, cq, 0, ("second",)))
    chunks.append((4, memory, kv, 0, ("memory",)))
    chunks.append((4, memory, kv, D, ()))
    chunks.append((5, ctx, branch, 0, ("ctx",)))
    for col in range(0, 3 * D, width):
        chunks.append((6, first, qkv, col, ("first",)))
    total = len(chunks)
    tall = {i: k for k, i in enumerate(BACK_TALL)}
    flat = {}
    ticks = []
    for i in range(total):
        if i in tall:
            ticks.append(len(flat) - 1)
        else:
            ticks.append(len(flat))
            flat[i] = len(flat)
    by_flat = {f: i for i, f in flat.items()}

    def products(i, core, emit):
        _, left, right, col, names = chunks[i]
        need(*names)
        own = left.shape[1] // grid.devices
        span = left.shape[1] // (n * CORES)
        lanes = width * rows // own

        band = min(lanes, 2 * BLOCK)

        def body(step, carry):
            yy, j = step // (lanes // band), step % (lanes // band)
            at = pl.multiple_of((yy * CORES + core) * span, min(span, BLOCK))
            value = transposed_times(
                left[:, pl.ds(at, span)],
                right[:, pl.ds(pl.multiple_of(col + j * band, BLOCK), band)],
            )
            for k in range(depth * n):
                for part in range(own // rows):
                    top = k * own + part * rows
                    lane = pl.multiple_of(part * lanes + j * band, BLOCK)
                    emit(yy, k // n, k % n, lane, band, value[top : top + rows])
            return carry

        lax.fori_loop(0, n * (lanes // band), body, 0)

    def reuse(i, stage, ring):
        before = i - ring if stage == 0 else by_flat.get(flat[i] - ring, -1)
        if before >= 0:
            for copy in copies[before, stage]:
                copy.wait_send()

    def credit(i):
        if i + RING < total:
            pl.semaphore_signal(free, inc=1, device_id=grid.partner(), device_id_type=MESH)

    def stage0(i):
        s = i % SPARE
        reuse(i, 0, SPARE)

        def emit(yy, zz, xx, lane, lanes, value):
            send0[s, yy, zz, xx, :, pl.ds(lane, lanes)] = value.astype(bf16)

        products(i, 1 - c, emit)
        if i >= RING:
            pl.semaphore_wait(free, 1)
        copies[i, 0] = [started(send0.at[s], got0.at[i % RING], s0.at[s], r0.at[i % RING], grid.partner())]

    def relative(yy, xx):
        to_y = lax.rem(yy - y + n, n)
        to_x = lax.rem(xx - x + n, n)
        return to_x * (1 - c) + to_y * c, to_y * (1 - c) + to_x * c

    def stage1(i):
        s, g = flat[i] % RING, i % RING
        reuse(i, 1, RING)
        copies[i, 0][0].wait_recv()

        def emit(yy, zz, xx, lane, lanes, value):
            value = value + got0[g, yy, zz, xx, :, pl.ds(lane, lanes)].astype(f32)
            a, b = relative(yy, xx)
            parts[s, a, b, zz, :, pl.ds(lane, lanes)] = value.astype(bf16)

        products(i, c, emit)
        credit(i)
        copies[i, 1] = []
        for a in range(1, n):
            if flat[i] >= RING:
                pl.semaphore_wait(free1.at[a - 1], 1)
            copies[i, 1].append(
                started(
                    parts.at[s, a],
                    got1.at[s, a - 1],
                    s1.at[s, a - 1],
                    r1.at[s, a - 1],
                    grid.step_plane(a, 0),
                )
            )

    def stage2(i):
        s, f = flat[i] % RING, flat[i]
        reuse(i, 2, RING)
        for copy in copies[i, 1]:
            copy.wait_recv()
        copies[i, 2] = []
        for b in list(range(1, n)) + [0]:

            def body(zz, carry):
                value = parts[s, 0, b, zz].astype(f32)
                for a in range(1, n):
                    value = value + got1[s, a - 1, b, zz].astype(f32)
                halves[s, b, zz] = value.astype(bf16)
                return carry

            lax.fori_loop(0, depth, body, 0)
            if b:
                copies[i, 2].append(
                    started(
                        halves.at[s, b],
                        got2.at[f, b - 1],
                        s2.at[s, b - 1],
                        r2.at[f, b - 1],
                        grid.step_plane(b, 1),
                    )
                )
        if f + RING < len(flat):
            for a in range(1, n):
                pl.semaphore_signal(
                    free1.at[a - 1], inc=1, device_id=grid.step_plane(n - a, 0), device_id_type=MESH
                )

    def stage3(i):
        s, f = flat[i] % RING, flat[i]
        reuse(i, 3, RING)
        for copy in copies[i, 2]:
            copy.wait_recv()

        def body(zz, carry):
            value = halves[s, 0, zz].astype(f32)
            for b in range(1, n):
                value = value + got2[f, b - 1, zz].astype(f32)
            line[s, zz] = value.astype(bf16)
            return carry

        lax.fori_loop(0, depth, body, 0)
        copies[i, 3] = [
            started(
                line.at[s, lax.rem(z + k, depth)],
                got3.at[f, k - 1],
                s3.at[s, k - 1],
                r3.at[f, k - 1],
                grid.step_z(k),
            )
            for k in range(1, depth)
        ]

    def tall1(i):
        k, g = tall[i], i % RING
        copies[i, 0][0].wait_recv()

        def emit(yy, zz, xx, lane, lanes, value):
            value = value + got0[g, yy, zz, xx, :, pl.ds(lane, lanes)].astype(f32)
            tower[k, zz, yy, xx, :, pl.ds(lane, lanes)] = value.astype(bf16)

        products(i, c, emit)
        credit(i)

    def level(up):
        return z if up else depth - 1 - z

    def pass_on(i, up, d):
        k = tall[i]
        target = lax.rem(z + (d if up else depth - d), depth)
        slot = target if up or d > 1 else depth
        to = grid.device(y, c, lax.rem(z + (1 if up else depth - 1), depth), x)
        return remote(
            tower.at[k, target], tower_got.at[k, slot], sz.at[k, target], rz.at[k, slot], to
        )

    def absorb(i, target, slot):
        k = tall[i]
        remote(
            tower.at[k, target], tower_got.at[k, slot], sz.at[k, target], rz.at[k, slot], grid.partner()
        ).wait_recv()

        def body(j, carry):
            yy, xx = j // n, j % n
            value = tower[k, target, yy, xx].astype(f32) + tower_got[k, slot, yy, xx].astype(f32)
            tower[k, target, yy, xx] = value.astype(bf16)
            return carry

        lax.fori_loop(0, n * n, body, 0)

    def tall_z(i, d):
        for up in (True, False):

            @pl.when(level(up) + d < depth)
            def _():
                target = lax.rem(z + (d if up else depth - d), depth)

                @pl.when(level(up) > 0)
                def _():
                    absorb(i, target, target)

                pass_on(i, up, d).start()

    def tall_plane(i):
        k = tall[i]

        @pl.when(z > 0)
        def _():
            absorb(i, z, z)

        @pl.when(z < depth - 1)
        def _():
            absorb(i, z, depth)

        copies[i, 1] = []
        for a in range(1, n):
            for b in range(n):
                yy, xx = grid.place(a, b)
                j = (a - 1) * n + b
                copies[i, 1].append(
                    started(
                        tower.at[k, z, yy, xx],
                        tower_got1.at[k, j],
                        sa.at[k, j],
                        ra.at[k, j],
                        grid.step_plane(a, 0),
                    )
                )

    def tall_half(i):
        k = tall[i]
        for copy in copies[i, 1]:
            copy.wait_recv()
        copies[i, 2] = []
        for b in list(range(1, n)) + [0]:
            yy, xx = grid.place(0, b)
            value = tower[k, z, yy, xx].astype(f32)
            for a in range(1, n):
                value = value + tower_got1[k, (a - 1) * n + b].astype(f32)
            tower_half[k, b] = value.astype(bf16)
            if b:
                copies[i, 2].append(
                    started(
                        tower_half.at[k, b],
                        tower_got2.at[k, b - 1],
                        sb.at[k, b - 1],
                        rb.at[k, b - 1],
                        grid.step_plane(b, 1),
                    )
                )

    def tall_out(i):
        k = tall[i]
        for copy in copies[i, 2]:
            copy.wait_recv()
        value = tower_half[k, 0].astype(f32)
        for b in range(1, n):
            value = value + tower_got2[k, b - 1].astype(f32)
        put_out(i, value)

    def put_out(i, value):
        m, left, _, col, _ = chunks[i]
        own = left.shape[1] // grid.devices
        if own == rows:
            grad_outs[m][:, pl.ds(col, width)] = value
        else:
            for part in range(own // rows):
                grad_outs[m][pl.ds(part * rows, rows), pl.ds(col, BLOCK)] = value[
                    :, part * BLOCK : (part + 1) * BLOCK
                ]

    def stage4(i):
        for copy in copies[i, 3]:
            copy.wait_recv()
        value = line[flat[i] % RING, z].astype(f32)
        for k in range(1, depth):
            value = value + got3[flat[i], k - 1].astype(f32)
        put_out(i, value)

    moves = [
        [grid.partner()],
        [grid.step_plane(a, 0) for a in range(1, n)],
        [grid.step_plane(a, 1) for a in range(1, n)],
        [grid.step_z(k) for k in range(1, depth)],
        [],
    ]
    start = [0, 1, n, 2 * n - 1, 2 * n + depth - 2]

    def gain_step(h):
        value = gain_sum[min(h, 3)]
        if h:
            for j, copy in enumerate(copies["gain", h - 1]):
                copy.wait_recv()
                value = value + gain_got[start[h - 1] + j]
        if h == len(moves) - 1:
            gain_out[...] = value
        elif h:
            gain_sum[h] = value
        if h < len(moves) - 2:
            gain_sum[h + 1] = value
        copies["gain", h] = [
            started(
                gain_sum.at[h],
                gain_got.at[start[h] + j],
                gs.at[start[h] + j],
                gr.at[start[h] + j],
                device,
            )
            for j, device in enumerate(moves[h])
        ]

    def context_grad(weight, col):
        g_ctx[...] = times_transposed(branch[...], weight[:, pl.ds(col, D)]).astype(bf16)

    lane = lax.broadcasted_iota(jnp.int32, (length, 2 * HD), 1)
    scale = HD ** (-0.5)

    def attention(page, pair, q_ref, q_col, k_ref, k_row, k_rows, k_col, v_col, lse, allowed):
        q_at = pl.ds(page * length, length)
        k_at = pl.ds(k_row, k_rows)
        q = both_heads(lane, q_ref[q_at, lane_window(q_col, pair)])
        g = both_heads(lane, g_ctx[q_at, lane_window(0, pair)])
        keys, values = k_ref[k_at, lane_window(k_col, pair)], k_ref[k_at, lane_window(v_col, pair)]
        scores = times_transposed(keys, q) * scale
        scores = jnp.where(allowed, scores, -1000000000.0)
        probs = jnp.exp(scores - lse[pl.ds(page * (D // HD // 2) + pair, 1), :])
        g_probs = times_transposed(values, g)
        inner = jnp.sum(probs * g_probs, axis=0, keepdims=True)
        g_scores = (probs * (g_probs - inner)).astype(bf16)
        g_values = times(probs.astype(bf16), g)
        g_keys = times(g_scores, q) * scale
        g_q = transposed_times(g_scores, keys)
        g_q = jnp.where(lane < HD, g_q[:length], g_q[length:]) * scale
        q_ref[q_at, lane_window(q_col, pair)] = g_q.astype(bf16)
        k_ref[k_at, lane_window(k_col, pair)] = g_keys.astype(bf16)
        k_ref[k_at, lane_window(v_col, pair)] = g_values.astype(bf16)

    def cross_attention(page):
        need("cq", "kv")
        place = lax.broadcasted_iota(jnp.int32, (slots, 2 * length), 0)
        allowed = place < counts[page]

        def body(pair, carry):
            attention(page, pair, cq, 0, kv, page * slots, slots, 0, D, lse_cross, allowed)
            return carry

        lax.fori_loop(0, D // (2 * HD), body, 0, unroll=2)

    def self_attention(page):
        need("qkv")
        allowed = causal(length, lengths[page])

        def body(pair, carry):
            attention(page, pair, qkv, 0, qkv, page * length, length, D, 2 * D, lse_self, allowed)
            return carry

        lax.fori_loop(0, D // (2 * HD), body, 0)

    def norm_back(value_ref, gain_row, put):
        gain = gains[pl.ds(gain_row, 1), :]

        def body(k, total_):
            at = pl.ds(k * 32, 32)
            value = value_ref[at].astype(f32)
            centred = value - jnp.mean(value, axis=-1, keepdims=True)
            spread = jnp.mean(centred * centred, axis=-1, keepdims=True)
            row_scale = lax.rsqrt(spread + EPS)
            unit = centred * row_scale
            grad = g_norm[at]
            grad_unit = grad * gain
            inner = jnp.mean(grad_unit * unit, axis=-1, keepdims=True)
            put(at, row_scale * (grad_unit - jnp.mean(grad_unit, axis=-1, keepdims=True) - unit * inner))
            return total_ + jnp.sum(grad * unit, axis=0, keepdims=True)

        summed = lax.fori_loop(0, value_ref.shape[0] // 32, body, jnp.zeros((1, D), f32))
        gain_sum[0, pl.ds(gain_row, 1), :] = summed

    def spread(terms):
        def body(k, carry):
            at = pl.ds(pl.multiple_of(k * 2 * BLOCK, BLOCK), 2 * BLOCK)
            value = None
            for left, left_col, right, right_col in terms:
                term = times_transposed(
                    left[:, pl.ds(left_col, D)], right[at, pl.ds(right_col, D)]
                )
                value = term if value is None else value + term
            g_norm[:, at] = value
            return carry

        lax.fori_loop(0, D // (2 * BLOCK), body, 0)

    def third_norm():
        need("pre", "out", "cross")
        need_all("expand")
        spread([(pre, 0, w_a, 0), (pre, D, w_a, D), (pre, 2 * D, w_b, 0), (pre, 3 * D, w_b, D)])

        def put(at, value):
            value = out_grad[at].astype(f32) + value
            cross[at] = value
            branch[at] = value.astype(bf16)

        norm_back(cross, 2, put)
        weights("qo", ("qo", 1, w_a, 1), ("qo", 0, w_a, 0))
        weights("self", ("self", 3, w_b, 0), ("self", 0, w_b, 1))

    def second_norm():
        need("self")
        fetch("x", x_in, third, 14)
        spread([(cq, 0, w_a, 0)])

        def put(at, value):
            value = cross[at] + value
            cross[at] = value
            branch[at] = value.astype(bf16)

        norm_back(after_self, 1, put)
        weights("pair", ("self", 1, w_a, 0), ("self", 2, w_a, 1))

    def first_norm():
        need("x")
        need_all("pair")
        spread([(qkv, 0, w_b, D), (qkv, D, w_a, 0), (qkv, 2 * D, w_a, D)])

        def put(at, value):
            input_out[at] = cross[at] + value

        norm_back(third, 0, put)
        weights("kv", ("kv", 0, w_b, 0), ("kv", 1, w_b, 1))

    def memory_grad(page, part):
        need_all("kv")
        slot = part % 2
        need(("stage", slot))
        top = part * span
        height = min(slots - top, span)
        live = min(memory_rows - top, height)
        at = pl.ds(page * slots + top, height)

        def body(k, carry):
            col = pl.multiple_of(k * BLOCK, BLOCK)
            value = times_transposed(kv[at, :], w_b[pl.ds(col, BLOCK), :])
            for j in range(BLOCK // 128):
                stage[slot, pl.ds(k * (BLOCK // 128) + j, live, 8), :] = value[:live, j * 128 : j * 128 + 128]
            return carry

        lax.fori_loop(0, D // BLOCK, body, 0)
        fetch(
            ("stage", slot),
            stage.at[slot, pl.ds(0, live * 8)],
            memory_out.at[pl.ds((page * memory_rows + top) * 8, live * 8)],
            19 + slot,
        )

    span = -(-slots // 32) * 16
    memory_rows = memory_out.shape[0] // 8 // pages
    gain_sum[0] = jnp.zeros(gain_sum.shape[1:], f32)
    plan = Plan()
    for i in range(total):
        t = ticks[i]
        plan.add(t - 2, 0, stage0, i)
        if i in tall:
            plan.add(t, 1, tall1, i)
            for d in range(depth - 1, 0, -1):
                plan.add(t + TALL_STEP * (depth - 1 - d), 5, tall_z, i, d)
            t += TALL_STEP * (depth - 1)
            plan.add(t, 5, tall_plane, i)
            plan.add(t + 1, 5, tall_half, i)
            plan.add(t + 2, 5, tall_out, i)
        else:
            plan.add(t, 1, stage1, i)
            plan.add(t + 1, 2, stage2, i)
            plan.add(t + 2, 3, stage3, i)
            plan.add(t + 3, 4, stage4, i)

    def cross_in_grad():
        need_all("qo")
        context_grad(w_a, D)

    def self_in_grad():
        need_all("self")
        context_grad(w_b, 0)

    plan.add(0, 9, third_norm)
    plan.add(1, 9, cross_in_grad)
    for page in range(pages):
        plan.add(1 + page, 10, cross_attention, page)
    turn = ticks[OUT_CHUNK]
    plan.add(turn, 8, second_norm)
    plan.add(turn, 9, self_in_grad)
    for page in range(pages):
        plan.add(turn + page, 11, self_attention, page)
    plan.add(turn + pages, 9, first_norm)
    for page in range(pages):
        for part in range(2):
            plan.add(turn + pages + 1 + 2 * part, 9, memory_grad, page, part)
    for h in range(len(moves)):
        plan.add(len(flat) - 4 + h, 7, gain_step, h)
    plan.run()
    for i in range(total):
        if i >= total - SPARE:
            copies[i, 0][0].wait_send()
        if i in tall:
            for copy in copies[i, 1] + copies[i, 2]:
                copy.wait_send()
            for up in (True, False):
                for d in range(1, depth):

                    @pl.when(level(up) + d < depth)
                    def _():
                        pass_on(i, up, d).wait_send()

        elif flat[i] >= len(flat) - RING:
            for stage in (1, 2, 3):
                for copy in copies[i, stage]:
                    copy.wait_send()
    for h in range(len(moves)):
        for copy in copies["gain", h]:
            copy.wait_send()
    need(*list(loads))


def backward(big, small, shapes):
    dp, fsdp = lax.axis_size("dp"), lax.axis_size("fsdp")
    n = dp // CORES
    depth = fsdp // n
    devices = dp * fsdp
    rows = WIDTH // devices
    pages, length, slots, live = shapes
    tokens = pages * length
    D = WIDTH
    high = len(BACK_TALL)
    t = sum(k * m for k, m in ((big[0].shape[1], D), (D, big[1].shape[1]), (D, 8 * D))) // (D * D) - high
    dma = pltpu.SemaphoreType.DMA
    hops = 2 * n + depth - 2
    outs = [(big[0].shape[1], D), (D, big[1].shape[1]), (D, D), (D, D), (D, 2 * D), (D, D), (D, 3 * D)]
    f32 = jnp.float32

    def scratch(*lead):
        return pltpu.VMEM(lead + (rows, WIDTH), jnp.bfloat16)

    def like(value):
        return pltpu.VMEM(value.shape, value.dtype)

    hbm = pl.BlockSpec(memory_space=pltpu.HBM)
    vmem = pl.BlockSpec(memory_space=pltpu.VMEM)
    smem = pl.BlockSpec(memory_space=pltpu.SMEM)
    return pl.pallas_call(
        functools.partial(back_kernel, (pages, length, slots)),
        out_shape=[jax.ShapeDtypeStruct((k // devices, m), f32) for k, m in outs]
        + [
            jax.ShapeDtypeStruct((8, D), f32),
            jax.ShapeDtypeStruct((tokens, D), f32),
            jax.ShapeDtypeStruct((pages * live * D // 128, 128), f32),
        ],
        in_specs=[hbm] * len(big) + [smem, smem] + [vmem] * 3,
        out_specs=[vmem] * (len(outs) + 2) + [hbm],
        scratch_shapes=[like(v) for v in big[:14]]
        + [pltpu.VMEM((D, 2 * D), jnp.bfloat16)] * 2
        + [pltpu.VMEM((tokens, D), jnp.bfloat16)] * 2
        + [
            pltpu.VMEM((2, -(-slots // 32) * 16 * 8, 128), f32),
            pltpu.VMEM((tokens, D), f32),
            scratch(SPARE, n, depth, n),
            scratch(RING, n, depth, n),
            scratch(RING, n, n, depth),
            scratch(RING, n - 1, n, depth),
            scratch(RING, n, depth),
            scratch(t, n - 1, depth),
            scratch(RING, depth),
            scratch(t, depth - 1),
            pltpu.VMEM((4, 8, D), f32),
            pltpu.VMEM((hops, 8, D), f32),
            scratch(high, depth, n, n),
            scratch(high, depth + 1, n, n),
            scratch(high, (n - 1) * n),
            scratch(high, n),
            scratch(high, n - 1),
            dma((21,)),
            dma((SPARE,)),
            dma((RING,)),
            dma((RING, n - 1)),
            dma((RING, n - 1)),
            dma((RING, n - 1)),
            dma((t, n - 1)),
            dma((RING, depth - 1)),
            dma((t, depth - 1)),
            dma((hops,)),
            dma((hops,)),
            pltpu.SemaphoreType.REGULAR,
            pltpu.SemaphoreType.REGULAR((n - 1,)),
            dma((high, depth)),
            dma((high, depth + 1)),
            dma((high, (n - 1) * n)),
            dma((high, (n - 1) * n)),
            dma((high, n - 1)),
            dma((high, n - 1)),
        ],
        compiler_params=pltpu.CompilerParams(
            collective_id=1, has_side_effects=True, vmem_limit_bytes=67043328
        ),
    )(*big, *small)


def hand_kernel(slabs, count, *refs):
    ins, gains = refs[:count], refs[count]
    outs, gain_outs = refs[count + 1 : 2 * count + 1], refs[2 * count + 1 : 2 * count + 4]
    buffers = refs[2 * count + 4 : 3 * count + 4]
    loaded, stored = refs[3 * count + 4 :]
    copies = []
    for k, (m, first, rows) in enumerate(slabs):
        at = pl.ds(first, rows)
        load = pltpu.make_async_copy(ins[m].at[at], buffers[m].at[at], loaded.at[k])
        load.start()
        copies.append((load, pltpu.make_async_copy(buffers[m].at[at], outs[m].at[at], stored.at[k])))
    entries = gain_outs[0].shape[-1]
    me = lax.axis_index("dp") * lax.axis_size("fsdp") + lax.axis_index("fsdp")
    turned = pltpu.roll(gains[...], lax.rem(gains.shape[1] - me * entries, gains.shape[1]), 1)
    for k, gain_out in enumerate(gain_outs):
        gain_out[...] = turned[k : k + 1, :entries]
    for load, store in copies:
        load.wait()
        store.start()
    for _, store in copies:
        store.wait()


def hand_over(arrays, gains):
    devices = lax.axis_size("dp") * lax.axis_size("fsdp")
    entries = gains.shape[1] // devices
    slabs = []
    for m, value in enumerate(arrays):
        parts = 4 if value.shape[0] % 64 == 0 and value.size >= 1 << 20 else 1
        rows = value.shape[0] // parts
        slabs += [(m, k * rows, rows) for k in range(parts)]
    hbm = pl.BlockSpec(memory_space=pltpu.HBM)
    vmem = pl.BlockSpec(memory_space=pltpu.VMEM)
    dma = pltpu.SemaphoreType.DMA
    found = pl.pallas_call(
        functools.partial(hand_kernel, slabs, len(arrays)),
        out_shape=[jax.ShapeDtypeStruct(v.shape, v.dtype) for v in arrays]
        + [jax.ShapeDtypeStruct((1, entries), gains.dtype)] * 3,
        in_specs=[hbm] * len(arrays) + [vmem],
        out_specs=[hbm] * len(arrays) + [vmem] * 3,
        scratch_shapes=[pltpu.VMEM(v.shape, v.dtype) for v in arrays]
        + [dma((len(slabs),)), dma((len(slabs),))],
        compiler_params=pltpu.CompilerParams(vmem_limit_bytes=67043328),
    )(*arrays, gains)
    return found[:-3], [v.reshape(-1) for v in found[-3:]]


def per_device(
    hidden_in,
    memory,
    cotangent,
    lengths,
    memory_count,
    causal_gain,
    causal_query,
    causal_key,
    causal_value,
    causal_output,
    source_gain,
    source_query,
    source_key,
    source_value,
    source_output,
    dense_gain,
    dense_expand,
    dense_reduce,
):
    pages, _, rows, width = hidden_in.shape
    slots = memory.shape[2]
    pad = -slots % 16
    source = jnp.pad(memory[:, 0], ((0, 0), (0, pad), (0, 0)))

    def flat(value):
        return value.reshape(pages * value.shape[1], value.shape[2])

    gains = jnp.stack([causal_gain, source_gain, dense_gain], axis=1)
    gains = jnp.pad(gains, ((0, 0), (0, 125)))
    sources = [
        causal_query,
        causal_key,
        causal_value,
        causal_output,
        source_key,
        source_value,
        source_query,
        source_output,
        dense_expand,
        dense_reduce,
        gains,
    ]
    names = [("gain", 0)]
    pieces = [(10, 0, 0, 0, False)]
    for first, count, name in ((4, 2, "kv"), (0, 4, "self"), (6, 2, "qo")):
        for k in range(count):
            pieces.append((first + k, 0, 0, len(names), False))
            names.append((name, k))
    for k in range(4):
        pieces.append((9, k * causal_query.shape[0], 0, len(names), k < 3))
    names.append(("reduce", 0))
    for k in range(4):
        pieces.append((8, 0, k * width, len(names), False))
        names.append(("expand", k))
    tokens = flat(hidden_in[:, 0])
    branch = flat(cotangent[:, 0])
    memory_rows = flat(source)
    page_length, page_count = lengths[:, 0], memory_count[:, 0]
    weights, saved, small = front(
        sources,
        pieces,
        names,
        [tokens, branch, memory_rows, page_count, page_length],
        (pages, rows, slots + pad),
    )
    result, hidden, pre, third, after_cross, cctx, second, cq, kv, after_self, ctx, first, qkv = saved
    gain_rows, lse_cross, lse_self = small
    big = [
        hidden,
        pre,
        third,
        branch,
        after_cross,
        cctx,
        second,
        cq,
        kv,
        memory_rows,
        after_self,
        ctx,
        first,
        qkv,
        tokens,
    ]
    place = {name: weight for name, weight in zip(names, weights)}
    big += [place[name, k] for name, count in KEPT for k in range(count)]
    small = [page_count, page_length, gain_rows, lse_cross, lse_self]
    (
        grad_reduce,
        grad_expand,
        grad_source_output,
        grad_source_query,
        grad_source_both,
        grad_causal_output,
        grad_causal,
        grad_gains,
        grad_inputs,
        grad_memory,
    ) = backward(big, small, (pages, rows, slots + pad, slots))
    (
        result,
        grad_inputs,
        grad_memory,
        grad_reduce,
        grad_expand,
        grad_source_output,
        grad_source_query,
        grad_source_both,
        grad_causal_output,
        grad_causal,
    ), grad_gains = hand_over(
        [
            result,
            grad_inputs,
            grad_memory,
            grad_reduce,
            grad_expand,
            grad_source_output,
            grad_source_query,
            grad_source_both,
            grad_causal_output,
            grad_causal,
        ],
        grad_gains,
    )
    return (
        result.reshape(hidden_in.shape),
        grad_inputs.reshape(pages, 1, rows, width),
        grad_memory.reshape(memory.shape),
        grad_gains[0],
        grad_causal[:, :width],
        grad_causal[:, width : 2 * width],
        grad_causal[:, 2 * width :],
        grad_causal_output,
        grad_gains[1],
        grad_source_query,
        grad_source_both[:, :width],
        grad_source_both[:, width:],
        grad_source_output,
        grad_gains[2],
        grad_expand,
        grad_reduce,
    )


def solution(mesh):
    pages = P(None, AXES, None, None)
    counts = P(None, AXES)
    gain = P(AXES)
    weight = P(AXES, None)
    return jax.shard_map(
        per_device,
        mesh=mesh,
        in_specs=(pages, pages, pages, counts, counts)
        + (gain, weight, weight, weight, weight)
        + (gain, weight, weight, weight, weight)
        + (gain, weight, weight),
        out_specs=(pages, pages, pages)
        + (gain, weight, weight, weight, weight)
        + (gain, weight, weight, weight, weight)
        + (gain, weight, weight),
        check_vma=False,
    )
```

profile of v0, /device:TPU:0, one launch (start us, length us, event | category | flops | bytes accessed | tf_op | source)
XLA Modules:
  0.0 324.9 jit_solution(17567452617081734932)
XLA Ops:
  0.6 0.7 pad_maximum_fusion
  1.3 0.1 copy.48
  1.4 0.6 pad.8.refs_10_
  2.1 2.4 copy.53
  4.5 1.7 pad.9.clone
  6.1 162.3 %shard_map.297 = (bf16[2,2,4,2,32,128]{5,4,3,2,1,0:T(8,128)(2,1)}, bf16[2,2,4,2,32,1024]{5,4,3,2,1,0:T(8,128)(2,1)}, bf16[2,2,4,2,32,1024]{5,4,3,2,1,0:T(8,128)(...) custom-call(bf16[32,1024]{1,0:T(8,128)(2,1)} %refs_0_.1, ...), custom_call_target="tpu_custom_call" | custom-call | tf_op jit(solution)/shard_map/pallas_call | solution.py:649
  168.4 146.8 %shard_map.298 = (f32[128,1024]{1,0:T(8,128)}, f32[32,4096]{1,0:T(8,128)}, f32[32,1024]{1,0:T(8,128)}, f32[32,1024]{1,0:T(8,128)}, f32[32,2048]{1,0:T(8,128)}, /...) custom-call(bf16[256,4096]{1,0:T(8,128)(2,1)} %get-tuple-element.68., ...), custom_call_target="tpu_custom_call" | custom-call | tf_op jit(solution)/shard_map/pallas_call | solution.py:1305
  315.3 7.7 %shard_map.299 = (bf16[256,1024]{1,0:T(8,128)(2,1)}, f32[256,1024]{1,0:T(8,128)}, f32[9408,128]{1,0:T(8,128)}, f32[128,1024]{1,0:T(8,128)}, f32[32,4096]{1,0:T(8...) custom-call(bf16[256,1024]{1,0:T(8,128)(2,1)} %get-tuple-element.67., ...), custom_call_target="tpu_custom_call" | custom-call | tf_op jit(solution)/shard_map/pallas_call | solution.py:1396
  322.9 2.0 fusion
where the time goes:
time: 326 us; the launch traced here: 325 us
  Pallas kernels  317 us (97%)
  local copies, waits for them, and re-layouts  6.79 us (2%)
    pallas_call x1, Pallas kernels, front(): pl.pallas_call(functools.partial(front_kernel, shapes, chunks, names, len...  162 us
    pallas_call x1, Pallas kernels, backward(): pl.pallas_call(functools.partial(back_kernel, (pages, length, slots)), ou...  147 us
    pallas_call x1, Pallas kernels, hand_over(): pl.pallas_call(functools.partial(hand_kernel, slabs, len(arrays)), out_sh...  7.68 us

commit v1 on v0

--- a/solution.py
+++ b/solution.py
@@ -153,7 +153,7 @@
 
 
 FLAT_AHEAD = 2
-TALL_GAP = 1
+TALL_GAP = 3
 
 
 def front_kernel(dims, chunks, names_, n_src, *refs):
@@ -535,11 +535,12 @@
     tall = [i for i, chunk in enumerate(chunks) if chunk[7]]
     tick = {}
     for t, i in enumerate(flat):
+        t = max(t - 1, 0)
         plan.add(t - FLAT_AHEAD, 0, stage_z, i)
         plan.add(t, 2, stage_p, i)
         plan.add(t + 1, 4, stage_q, i)
-        plan.add(t + 2, 6, stage_c, i)
-        tick[i] = t + 3
+        plan.add(t + 3, 6, stage_c, i)
+        tick[i] = t + 4
     for t, i in enumerate(tall):
         t = TALL_GAP * t - 1
         plan.add(t, 1, tall_p, i)
@@ -1359,50 +1360,55 @@
     )(*big, *small)
 
 
-def hand_kernel(slabs, count, *refs):
+def hand_kernel(slabs, count, made, *refs):
     ins, gains = refs[:count], refs[count]
-    outs, gain_outs = refs[count + 1 : 2 * count + 1], refs[2 * count + 1 : 2 * count + 4]
-    buffers = refs[2 * count + 4 : 3 * count + 4]
-    loaded, stored = refs[3 * count + 4 :]
-    copies = []
-    for k, (m, first, rows) in enumerate(slabs):
-        at = pl.ds(first, rows)
-        load = pltpu.make_async_copy(ins[m].at[at], buffers[m].at[at], loaded.at[k])
-        load.start()
-        copies.append((load, pltpu.make_async_copy(buffers[m].at[at], outs[m].at[at], stored.at[k])))
+    outs, gain_outs = refs[count + 1 : count + 1 + made], refs[count + 1 + made : count + 4 + made]
+    buffers = refs[count + 4 + made : 2 * count + 4 + made]
+    loaded, stored = refs[2 * count + 4 + made :]
+    loads, stores = [], []
+    for k, (m, rows, pieces) in enumerate(slabs):
+        at = pl.ds(*rows)
+        loads.append(pltpu.make_async_copy(ins[m].at[at], buffers[m].at[at], loaded.at[k]))
+        loads[-1].start()
     entries = gain_outs[0].shape[-1]
     me = lax.axis_index("dp") * lax.axis_size("fsdp") + lax.axis_index("fsdp")
     turned = pltpu.roll(gains[...], lax.rem(gains.shape[1] - me * entries, gains.shape[1]), 1)
     for k, gain_out in enumerate(gain_outs):
         gain_out[...] = turned[k : k + 1, :entries]
-    for load, store in copies:
+    for load, (m, rows, pieces) in zip(loads, slabs):
         load.wait()
-        store.start()
-    for _, store in copies:
+        at = pl.ds(*rows)
+        for o, col in pieces:
+            src = buffers[m].at[at, pl.ds(col, outs[o].shape[1])]
+            stores.append(pltpu.make_async_copy(src, outs[o].at[at], stored.at[len(stores)]))
+            stores[-1].start()
+    for store in stores:
         store.wait()
 
 
 def hand_over(arrays, gains):
     devices = lax.axis_size("dp") * lax.axis_size("fsdp")
     entries = gains.shape[1] // devices
-    slabs = []
-    for m, value in enumerate(arrays):
-        parts = 4 if value.shape[0] % 64 == 0 and value.size >= 1 << 20 else 1
-        rows = value.shape[0] // parts
-        slabs += [(m, k * rows, rows) for k in range(parts)]
+    slabs, outs = [], []
+    for m, (value, parts) in enumerate(arrays):
+        cols = value.shape[1] // parts
+        pieces = [(len(outs) + k, k * cols) for k in range(parts)]
+        outs += [jax.ShapeDtypeStruct((value.shape[0], cols), value.dtype)] * parts
+        cuts = 4 if value.shape[0] % 64 == 0 and value.size >= 1 << 20 else 1
+        rows = value.shape[0] // cuts
+        slabs += [(m, (k * rows, rows), pieces) for k in range(cuts)]
     hbm = pl.BlockSpec(memory_space=pltpu.HBM)
     vmem = pl.BlockSpec(memory_space=pltpu.VMEM)
     dma = pltpu.SemaphoreType.DMA
     found = pl.pallas_call(
-        functools.partial(hand_kernel, slabs, len(arrays)),
-        out_shape=[jax.ShapeDtypeStruct(v.shape, v.dtype) for v in arrays]
-        + [jax.ShapeDtypeStruct((1, entries), gains.dtype)] * 3,
+        functools.partial(hand_kernel, slabs, len(arrays), len(outs)),
+        out_shape=outs + [jax.ShapeDtypeStruct((1, entries), gains.dtype)] * 3,
         in_specs=[hbm] * len(arrays) + [vmem],
-        out_specs=[hbm] * len(arrays) + [vmem] * 3,
-        scratch_shapes=[pltpu.VMEM(v.shape, v.dtype) for v in arrays]
-        + [dma((len(slabs),)), dma((len(slabs),))],
+        out_specs=[hbm] * len(outs) + [vmem] * 3,
+        scratch_shapes=[pltpu.VMEM(v.shape, v.dtype) for v, _ in arrays]
+        + [dma((len(slabs),)), dma((sum(len(pieces) for _, _, pieces in slabs),))],
         compiler_params=pltpu.CompilerParams(vmem_limit_bytes=67043328),
-    )(*arrays, gains)
+    )(*[v for v, _ in arrays], gains)
     return found[:-3], [v.reshape(-1) for v in found[-3:]]
 
 
@@ -1456,10 +1462,10 @@
             pieces.append((first + k, 0, 0, len(names), False))
             names.append((name, k))
     for k in range(4):
-        pieces.append((9, k * causal_query.shape[0], 0, len(names), k < 3))
+        pieces.append((9, k * causal_query.shape[0], 0, len(names), k < 2))
     names.append(("reduce", 0))
     for k in range(4):
-        pieces.append((8, 0, k * width, len(names), False))
+        pieces.append((8, 0, k * width, len(names), k == 3))
         names.append(("expand", k))
     tokens = flat(hidden_in[:, 0])
     branch = flat(cotangent[:, 0])
@@ -1507,44 +1513,43 @@
         grad_memory,
     ) = backward(big, small, (pages, rows, slots + pad, slots))
     (
+        grad_memory,
+        grad_inputs,
         result,
-        grad_inputs,
-        grad_memory,
         grad_reduce,
         grad_expand,
+        *grad_causal,
+        grad_source_key,
+        grad_source_value,
+        grad_source_query,
         grad_source_output,
-        grad_source_query,
-        grad_source_both,
         grad_causal_output,
-        grad_causal,
     ), grad_gains = hand_over(
         [
-            result,
-            grad_inputs,
-            grad_memory,
-            grad_reduce,
-            grad_expand,
-            grad_source_output,
-            grad_source_query,
-            grad_source_both,
-            grad_causal_output,
-            grad_causal,
+            (grad_memory, 1),
+            (grad_inputs, 1),
+            (result, 1),
+            (grad_reduce, 1),
+            (grad_expand, 1),
+            (grad_causal, 3),
+            (grad_source_both, 2),
+            (grad_source_query, 1),
+            (grad_source_output, 1),
+            (grad_causal_output, 1),
         ],
         grad_gains,
     )
     return (
         result.reshape(hidden_in.shape),
-        grad_inputs.reshape(pages, 1, rows, width),
+        grad_inputs.reshape(hidden_in.shape),
         grad_memory.reshape(memory.shape),
         grad_gains[0],
-        grad_causal[:, :width],
-        grad_causal[:, width : 2 * width],
-        grad_causal[:, 2 * width :],
+        *grad_causal,
         grad_causal_output,
         grad_gains[1],
         grad_source_query,
-        grad_source_both[:, :width],
-        grad_source_both[:, width:],
+        grad_source_key,
+        grad_source_value,
         grad_source_output,
         grad_gains[2],
         grad_expand,

time: 326 us -> 319 us (0.979)
  Pallas kernels: 317 us -> 312 us
    pallas_call x1, Pallas kernels: 162 us -> 153 us  [front(): pl.pallas_call(functools.partial(front_kernel, shapes, chunks, names, len...]
    pallas_call x1, Pallas kernels: 147 us -> 150 us  [backward(): pl.pallas_call(functools.partial(back_kernel, (pages, length, slots)), ou...]
where the time goes in v1:
time: 319 us; the launch traced here: 318 us
  Pallas kernels  312 us (98%)
  local copies, waits for them, and re-layouts  4.78 us (1%)
    pallas_call x1, Pallas kernels, front(): pl.pallas_call(functools.partial(front_kernel, shapes, chunks, names, len...  153 us
    pallas_call x1, Pallas kernels, backward(): pl.pallas_call(functools.partial(back_kernel, (pages, length, slots)), ou...  150 us
    pallas_call x1, Pallas kernels, hand_over(): pl.pallas_call(functools.partial(hand_kernel, slabs, len(arrays), len(out...  8.07 us

profile of v1, /device:TPU:0, one launch (start us, length us, event | category | flops | bytes accessed | tf_op | source)
XLA Modules:
  0.0 318.0 jit_solution(11047857349752426105)
XLA Ops:
  0.6 0.7 pad_maximum_fusion
  1.3 0.1 copy.48
  1.4 0.6 pad.8.refs_10_
  2.1 2.4 copy.53
  4.5 1.7 pad.9.clone
  6.1 153.3 %shard_map.297 = (bf16[2,2,4,2,32,128]{5,4,3,2,1,0:T(8,128)(2,1)}, bf16[2,2,4,2,32,1024]{5,4,3,2,1,0:T(8,128)(2,1)}, bf16[2,2,4,2,32,1024]{5,4,3,2,1,0:T(8,128)(...) custom-call(bf16[32,1024]{1,0:T(8,128)(2,1)} %refs_0_.1, ...), custom_call_target="tpu_custom_call" | custom-call | tf_op jit(solution)/shard_map/pallas_call | solution.py:650
  159.5 150.3 %shard_map.298 = (f32[128,1024]{1,0:T(8,128)}, f32[32,4096]{1,0:T(8,128)}, f32[32,1024]{1,0:T(8,128)}, f32[32,1024]{1,0:T(8,128)}, f32[32,2048]{1,0:T(8,128)}, /...) custom-call(bf16[256,4096]{1,0:T(8,128)(2,1)} %get-tuple-element.70., ...), custom_call_target="tpu_custom_call" | custom-call | tf_op jit(solution)/shard_map/pallas_call | solution.py:1306
  309.7 8.1 %shard_map.299 = (f32[9408,128]{1,0:T(8,128)}, f32[256,1024]{1,0:T(8,128)}, bf16[256,1024]{1,0:T(8,128)(2,1)}, f32[128,1024]{1,0:T(8,128)}, f32[32,4096]{1,0:T(8...) custom-call(f32[9408,128]{1,0:T(8,128)} %get-tuple-element.97.refs_0, ...), custom_call_target="tpu_custom_call" | custom-call | tf_op jit(solution)/shard_map/pallas_call | solution.py:1403
